TPU v7x, 32 devices: a whole 2x2x4 slice. The times are simulated.
32 devices in a mesh: section: 4 (over y, core), expert: 8 (over z, x).
Axes of the slice: x: 2, y: 2, z: 4, core: 2. Of those that a mesh axis runs over, the one named last changes fastest.
Arguments:
- tokens: bfloat16 [1024, 3584], P('expert', 'section'), may hold values from -6 to 6
- expert_ids: int32 [1024, 2], P('expert'), may hold values from 0 to 7, all different within a row; in each aligned block of 128 rows (0 to 127, 128 to 255, ...) at most 48 rows name the same one
- gates: float32 [1024, 2], P('expert'), may hold values from 0.02 to 0.4
- cotangent: bfloat16 [1024, 3584], P('expert', 'section'), may hold values from -6 to 6
- w_gate: bfloat16 [8, 3584, 1024], P('expert', 'section'), may hold values from -0.09375 to 0.09375
- w_up: bfloat16 [8, 3584, 1024], P('expert', 'section'), may hold values from -0.09375 to 0.09375
- w_down: bfloat16 [8, 1024, 3584], P('expert', None, 'section'), may hold values from -0.1875 to 0.1875
Outputs:
- mixed: bfloat16 [1024, 3584], P('expert', 'section')
- token_grads: bfloat16 [1024, 3584], P('expert', 'section')
- down_grads: bfloat16 [8, 1024, 3584], P('expert', None, 'section')
Inputs may be any that keep to these rules, and one draw needn't show every extreme that they name: `expert_ids`: within each aligned block of 128 rows no expert is named more than 48 times, a bound that some block reaches; the 2 experts of a row differ.
All inputs are finite; a program needn't handle non-finite values.
Results may differ from a plain program's by a relative error of at most 0.024.
Values may be sent and summed in bfloat16 or wider, within the bound.
A program may use at most 64 MiB of HBM per device.

v0:
```python
import jax
import jax.numpy as jnp
from jax import lax
from jax.sharding import PartitionSpec as P


def local(tokens, expert_ids, gates, cotangent, w_gate, w_up, w_down):
    tok_rows, top_count = expert_ids.shape
    col_span = tokens.shape[1]
    expert_count = lax.axis_size("expert")
    capacity = min(tok_rows, max(2, 3 * tok_rows * top_count // (2 * expert_count)))
    slot_total = expert_count * capacity
    one_hot = (
        expert_ids[:, :, None] == jnp.arange(expert_count, dtype=jnp.int32)[None, None, :]
    ).astype(jnp.int32)
    one_hot = one_hot.reshape(tok_rows * top_count, expert_count)
    earlier = jnp.cumsum(one_hot, axis=0) - one_hot
    ranks = jnp.sum(earlier * one_hot, axis=1)
    slot_ids = expert_ids.reshape(-1) * capacity + ranks
    picker = (slot_ids[:, None] == jnp.arange(slot_total, dtype=jnp.int32)[None, :]).astype(
        jnp.float32
    )
    picker_rows = picker.reshape(tok_rows, top_count, slot_total)
    chooser = jnp.sum(picker_rows, axis=1)
    weigher = jnp.sum(picker_rows * gates[:, :, None], axis=1)
    sent_rows = jnp.dot(
        chooser.T.astype(jnp.bfloat16), tokens, preferred_element_type=jnp.float32
    ).astype(jnp.bfloat16)
    sent_grads = jnp.dot(
        weigher.T, cotangent.astype(jnp.float32), precision=lax.Precision.HIGHEST
    ).astype(jnp.bfloat16)
    routed_rows, routed_grads = (
        lax.all_to_all(sent_rows, "expert", split_axis=0, concat_axis=0, tiled=True),
        lax.all_to_all(sent_grads, "expert", split_axis=0, concat_axis=0, tiled=True),
    )
    gate_w = w_gate[0]
    up_w = w_up[0]
    down_w = w_down[0]
    grad_term = jnp.einsum("rc,hc->rh", routed_grads, down_w, preferred_element_type=jnp.float32)
    gate_term = jnp.dot(routed_rows, gate_w, preferred_element_type=jnp.float32)
    up_term = jnp.dot(routed_rows, up_w, preferred_element_type=jnp.float32)
    gate_pre, up_pre, hidden_grad = (
        lax.psum_scatter(
            gate_term.astype(jnp.bfloat16), "section", scatter_dimension=1, tiled=True
        ).astype(jnp.float32),
        lax.psum_scatter(
            up_term.astype(jnp.bfloat16), "section", scatter_dimension=1, tiled=True
        ).astype(jnp.float32),
        lax.psum_scatter(
            grad_term.astype(jnp.bfloat16), "section", scatter_dimension=1, tiled=True
        ).astype(jnp.float32),
    )
    sigmoid_val = jax.nn.sigmoid(gate_pre)
    activated = gate_pre * sigmoid_val
    hidden = (activated * up_pre).astype(jnp.bfloat16)
    gate_grad = (
        hidden_grad * up_pre * sigmoid_val * (1.0 + gate_pre * (1.0 - sigmoid_val))
    ).astype(jnp.bfloat16)
    up_grad = (hidden_grad * activated).astype(jnp.bfloat16)
    full_hidden, full_gate_grad, full_up_grad = (
        lax.all_gather(hidden, "section", axis=1, tiled=True),
        lax.all_gather(gate_grad, "section", axis=1, tiled=True),
        lax.all_gather(up_grad, "section", axis=1, tiled=True),
    )
    out_rows = jnp.dot(full_hidden, down_w, preferred_element_type=jnp.float32).astype(jnp.bfloat16)
    down_grad = jnp.einsum(
        "rh,rc->hc", full_hidden, routed_grads, preferred_element_type=jnp.float32
    ).astype(jnp.bfloat16)
    slot_grad = jnp.einsum("rh,ch->rc", full_gate_grad, gate_w, preferred_element_type=jnp.float32)
    slot_grad = (
        slot_grad + jnp.einsum("rh,ch->rc", full_up_grad, up_w, preferred_element_type=jnp.float32)
    ).astype(jnp.bfloat16)
    back_out, back_grad = (
        lax.all_to_all(out_rows, "expert", split_axis=0, concat_axis=0, tiled=True),
        lax.all_to_all(slot_grad, "expert", split_axis=0, concat_axis=0, tiled=True),
    )
    picked_out = jnp.dot(picker.astype(jnp.bfloat16), back_out, preferred_element_type=jnp.float32)
    picked_out = picked_out.reshape(tok_rows, top_count, col_span)
    mixed = jnp.sum(gates[:, :, None] * picked_out, axis=1).astype(jnp.bfloat16)
    token_grads = jnp.dot(
        chooser.astype(jnp.bfloat16), back_grad, preferred_element_type=jnp.float32
    ).astype(jnp.bfloat16)
    return (mixed, token_grads, down_grad[None])


def solution(mesh):
    placed = (
        P("expert", "section"),
        P("expert", None),
        P("expert", None),
        P("expert", "section"),
        P("expert", "section", None),
        P("expert", "section", None),
        P("expert", None, "section"),
    )
    return jax.shard_map(
        local,
        mesh=mesh,
        in_specs=placed,
        out_specs=(P("expert", "section"), P("expert", "section"), P("expert", None, "section")),
        check_vma=False,
    )
```

profile of v0, /device:TPU:0, one launch (start us, length us, event | category | flops | bytes accessed | tf_op | source)
XLA Modules:
  0.0 190.6 jit_solution(15391791823256268737)
XLA Ops:
  7.2 0.0 copy-start
  7.2 0.0 reduce-scatter.4.cloned.1.call-start
  7.2 0.9 copy.24
  8.1 0.1 eq.64
  8.3 0.1 eq.60
  8.4 0.6 reduce-window.6
  9.0 0.2 slice_reduce_fusion
  9.3 0.1 fusion.46
  9.4 0.1 reduce_sum.39
  9.5 0.1 copy.26
  9.6 0.0 copy-start.4
  9.6 0.8 multiply_add_fusion
  10.4 0.8 select_reduce_fusion
  11.3 1.3 convolution_convert_fusion.1
  12.6 25.3 %all_to_all.48 = bf16[8,48,896]{2,1,0:T(8,128)(2,1)S(1)} all-to-all(bf16[8,48,896]{2,1,0:T(8,128)(2,1)S(1)} %bitcast.67), channel_id=1, replica_groups=mesh['section'=4,'expert'=8] {'expert'}, dimensions={0} | all-to-all | bytes 1376256 | tf_op jit(solution)/shard_map/all_to_all | solution.py:33
  37.9 0.0 copy-done.4
  37.9 1.9 fusion.15
  39.8 0.0 reduce-scatter.4.cloned.1.call-update
  39.8 0.0 copy-start.2
  39.8 0.0 reduce-scatter.6.cloned.1.call-start
  39.9 0.0 copy-done
  39.9 1.9 fusion.18
  41.7 0.0 reduce-scatter.6.cloned.1.call-update
  41.7 0.0 reduce-scatter.8.cloned.1.call-start
  41.8 0.0 copy-start.6
  41.8 0.0 copy-done.2
  41.8 0.8 convolution_convert_fusion
  42.6 21.3 %all_to_all.49 = bf16[8,48,896]{2,1,0:T(8,128)(2,1)S(1)} all-to-all(bf16[8,48,896]{2,1,0:T(8,128)(2,1)S(1)} %bitcast.66), channel_id=1, replica_groups=mesh['section'=4,'expert'=8] {'expert'}, dimensions={0} | all-to-all | bytes 1376256 | tf_op jit(solution)/shard_map/all_to_all | solution.py:34
  63.8 0.0 copy-start.1
  63.8 0.8 copy-done.1
  64.7 0.0 copy-done.6
  64.7 1.9 %fusion.21 = bf16[384,1024]{1,0:T(8,128)(2,1)} fusion(bf16[384,896]{1,0:T(8,128)(2,1)S(1)} %bitcast.68, bf16[1,1024,896]{2,1,0:T(8,128)(2,1)S(1)} %copy-done.6), kind=kOutput, calls=%fused_computation.16 | convolution fusion | flops 705036288 | bytes 3309568 | tf_op jit(solution)/shard_map/rc,hc->rh/dot_general | solution.py:39
  66.6 0.0 reduce-scatter.8.cloned.1.call-update
  66.6 0.0 reduce-scatter.4.cloned.1.call-done
  66.7 21.7 %reduce-scatter.6.cloned.1.call-done = bf16[384,256]{1,0:T(8,128)(2,1)} async-done(((bf16[384,1024]{1,0:T(8,128)(2,1)}), bf16[384,256]{1,0:T(8,128)(2,1)}) %reduce-scatter.6.cloned.1.call-update) | async-done | bytes 196624 | tf_op jit(solution)/shard_map/reduce_scatter | solution.py:46
  88.3 25.8 %reduce-scatter.8.cloned.1.call-done = bf16[384,256]{1,0:T(8,128)(2,1)} async-done(((bf16[384,1024]{1,0:T(8,128)(2,1)}), bf16[384,256]{1,0:T(8,128)(2,1)}) %reduce-scatter.8.cloned.1.call-update) | async-done | bytes 196624 | tf_op jit(solution)/shard_map/reduce_scatter | solution.py:49
  114.1 2.0 %fusion.34 = (bf16[384,256]{1,0:T(8,128)(2,1)S(1)}, bf16[384,256]{1,0:T(8,128)(2,1)S(1)}, bf16[384,256]{1,0:T(8,128)(2,1)}) fusion(bf16[384,256]{1,0:T(8,128)(2,1)} %reduce-scatter.6.cloned.1.call-done, bf16[384,256]{1,0:T(8,128)(2,1)} %reduce-scatter.8.cloned.1.call-done, bf16[384,256]{1,0:T(8,128)(2,1)} %reduce-scatter.4.cloned.1.call-done), kind=kLoop, calls=%fused_computation.33 | loop fusion | flops 1769472 | bytes 1179648 | tf_op jit(solution)/shard_map/convert_element_type | solution.py:58
  116.2 8.0 %all_gather.11 = bf16[384,1024]{1,0:T(8,128)(2,1)S(1)} all-gather(bf16[384,256]{1,0:T(8,128)(2,1)S(1)} %get-tuple-element.6), channel_id=1, replica_groups=mesh['section'=4,'expert'=8] {'section'}, dimensions={1}, use_global_device_ids=true | all-gather | bytes 983040 | tf_op jit(solution)/shard_map/all_gather | solution.py:63
  124.2 0.0 copy-start.5
  124.2 1.0 fusion.4
  125.2 8.7 %all_gather.10 = bf16[384,1024]{1,0:T(8,128)(2,1)S(1)} all-gather(bf16[384,256]{1,0:T(8,128)(2,1)S(1)} %get-tuple-element.5), channel_id=1, replica_groups=mesh['section'=4,'expert'=8] {'section'}, dimensions={1}, use_global_device_ids=true | all-gather | bytes 983040 | tf_op jit(solution)/shard_map/all_gather | solution.py:62
  133.9 0.0 copy-done.5
  133.9 1.9 fusion.24
  135.8 5.5 %all-to-all-start.3 = ((bf16[8,48,896]{2,1,0:T(8,128)(2,1)}), bf16[8,48,896]{2,1,0:T(8,128)(2,1)S(1)}, u32[]{:S(2)}, u32[]{:S(2)}) async-start(bf16[8,48,896]{2,1,0:T(8,128)(2,1)} %bitcast.13), calls=%async_computation.6 | async-start | bytes 1376256 | tf_op jit(solution)/shard_map/all_to_all | solution.py:75
  141.3 8.6 %all_gather.9 = bf16[384,1024]{1,0:T(8,128)(2,1)S(1)} all-gather(bf16[384,256]{1,0:T(8,128)(2,1)} %get-tuple-element.7), channel_id=1, replica_groups=mesh['section'=4,'expert'=8] {'section'}, dimensions={1}, use_global_device_ids=true | all-gather | bytes 983040 | tf_op jit(solution)/shard_map/all_gather | solution.py:61
  149.9 3.3 %fusion.27 = bf16[384,896]{1,0:T(8,128)(2,1)} fusion(bf16[384,1024]{1,0:T(8,128)(2,1)S(1)} %all_gather.9, bf16[1,1024,896]{2,1,0:T(8,128)(2,1)} %param.13), kind=kOutput, calls=%fused_computation.18 | convolution fusion | flops 704987136 | bytes 3309568 | tf_op jit(solution)/shard_map/dot_general | solution.py:65
  153.2 6.6 %all-to-all-done.3 = bf16[8,48,896]{2,1,0:T(8,128)(2,1)S(1)} async-done(((bf16[8,48,896]{2,1,0:T(8,128)(2,1)}), bf16[8,48,896]{2,1,0:T(8,128)(2,1)S(1)}, u32[]{:S(2)}, u32[]{:S(2)}) %all-to-all-start.3) | async-done | bytes 688160 | tf_op jit(solution)/shard_map/all_to_all | solution.py:75
  159.8 4.2 %all-to-all-start.1 = ((bf16[8,48,896]{2,1,0:T(8,128)(2,1)}), bf16[8,48,896]{2,1,0:T(8,128)(2,1)}, u32[]{:S(2)}, u32[]{:S(2)}) async-start(bf16[8,48,896]{2,1,0:T(8,128)(2,1)} %bitcast.70), calls=%async_computation.3 | async-start | bytes 1376256 | tf_op jit(solution)/shard_map/all_to_all | solution.py:74
  164.0 0.0 copy-start.3
  164.0 3.6 %convert_bitcast_fusion = bf16[1,1024,896]{2,1,0:T(8,128)(2,1)} fusion(bf16[384,1024]{1,0:T(8,128)(2,1)S(1)} %all_gather.9, bf16[384,896]{1,0:T(8,128)(2,1)} %bitcast.69), kind=kOutput, calls=%fused_computation.12 | convolution fusion | flops 705560576 | bytes 3309568 | tf_op jit(solution)/shard_map/rh,rc->hc/dot_general | solution.py:66
  167.6 1.0 convolution_convert_fusion.2
  168.6 13.2 %all-to-all-done.1 = bf16[8,48,896]{2,1,0:T(8,128)(2,1)} async-done(((bf16[8,48,896]{2,1,0:T(8,128)(2,1)}), bf16[8,48,896]{2,1,0:T(8,128)(2,1)}, u32[]{:S(2)}, u32[]{:S(2)}) %all-to-all-start.1) | async-done | bytes 688160 | tf_op jit(solution)/shard_map/all_to_all | solution.py:74
  181.8 0.0 copy-done.3
  181.8 2.3 %fusion.30 = bf16[128,896]{1,0:T(8,128)(2,1)} fusion(bf16[384,896,1]{1,0,2:T(8,128)(2,1)} %bitcast.10, f32[128,2]{0,1:T(2,128)S(1)} %copy-done.3, s32[128,2]{0,1:T(2,128)S(1)} %multiply_add_fusion), kind=kOutput, calls=%fused_computation.22 | convolution fusion | flops 176799744 | bytes 919552 | tf_op jit(solution)/shard_map/dot_general | solution.py:77
  (3 shorter events, 0.0 us)
Async XLA Ops:
  7.2 32.7 %copy-start = (bf16[1,896,1024]{2,1,0:T(8,128)(2,1)S(1)}, bf16[1,896,1024]{2,1,0:T(8,128)(2,1)}, u32[]{:S(2)}) copy-start(bf16[1,896,1024]{2,1,0:T(8,128)(2,1)} %param.12) | copy-start | bytes 5505028
  7.2 59.5 %reduce-scatter.4.cloned.1.call-start = ((), (), s32[]{:S(2)}) async-start(), calls=%async_computation.7 | async-start | bytes 983040 | tf_op jit(solution)/shard_map/reduce_scatter | solution.py:43
  9.6 28.3 %copy-start.4 = (bf16[1,896,1024]{2,1,0:T(8,128)(2,1)S(1)}, bf16[1,896,1024]{2,1,0:T(8,128)(2,1)}, u32[]{:S(2)}) copy-start(bf16[1,896,1024]{2,1,0:T(8,128)(2,1)} %param.11) | copy-start | bytes 5505028
  39.8 2.0 %copy-start.2 = (bf16[128,896]{1,0:T(8,128)(2,1)S(1)}, bf16[128,896]{1,0:T(8,128)(2,1)}, u32[]{:S(2)}) copy-start(bf16[128,896]{1,0:T(8,128)(2,1)} %param.10) | copy-start | bytes 688132
  39.8 48.5 %reduce-scatter.6.cloned.1.call-start = ((), (), s32[]{:S(2)}) async-start(), calls=%async_computation.8 | async-start | bytes 983040 | tf_op jit(solution)/shard_map/reduce_scatter | solution.py:46
  41.7 72.4 %reduce-scatter.8.cloned.1.call-start = ((), (), s32[]{:S(2)}) async-start(), calls=%async_computation.9 | async-start | bytes 983040 | tf_op jit(solution)/shard_map/reduce_scatter | solution.py:49
  41.8 22.9 %copy-start.6 = (bf16[1,1024,896]{2,1,0:T(8,128)(2,1)S(1)}, bf16[1,1024,896]{2,1,0:T(8,128)(2,1)}, u32[]{:S(2)}) copy-start(bf16[1,1024,896]{2,1,0:T(8,128)(2,1)} %param.13) | copy-start | bytes 5505028
  63.8 0.8 copy-start.1
  124.2 9.7 %copy-start.5 = (bf16[1,896,1024]{2,1,0:T(8,128)(2,1)S(1)}, bf16[1,896,1024]{2,1,0:T(8,128)(2,1)}, u32[]{:S(2)}) copy-start(bf16[1,896,1024]{2,1,0:T(8,128)(2,1)} %param.11) | copy-start | bytes 5505028
  135.8 24.0 %all-to-all-start.3 = ((bf16[8,48,896]{2,1,0:T(8,128)(2,1)}), bf16[8,48,896]{2,1,0:T(8,128)(2,1)S(1)}, u32[]{:S(2)}, u32[]{:S(2)}) async-start(bf16[8,48,896]{2,1,0:T(8,128)(2,1)} %bitcast.13), calls=%async_computation.6 | async-start | bytes 1376256 | tf_op jit(solution)/shard_map/all_to_all | solution.py:75
  159.8 22.0 %all-to-all-start.1 = ((bf16[8,48,896]{2,1,0:T(8,128)(2,1)}), bf16[8,48,896]{2,1,0:T(8,128)(2,1)}, u32[]{:S(2)}, u32[]{:S(2)}) async-start(bf16[8,48,896]{2,1,0:T(8,128)(2,1)} %bitcast.70), calls=%async_computation.3 | async-start | bytes 1376256 | tf_op jit(solution)/shard_map/all_to_all | solution.py:74
  164.0 17.8 %copy-start.3 = (f32[128,2]{0,1:T(2,128)S(1)}, f32[128,2]{0,1:T(2,128)}, u32[]{:S(2)}) copy-start(f32[128,2]{0,1:T(2,128)} %param.9) | copy-start | bytes 3076
Sparse Core Ops, SparseCore 0:
  39.9 22.0 reduce-scatter.3
  65.1 23.1 reduce-scatter.5
  90.9 23.1 reduce-scatter.7
where the time goes:
time: 191 us
  blocking collectives  71.9 us (38%)
  waiting for transfers between devices  67.3 us (35%)
  matrix products  20.8 us (11%)
  between operations  13.9 us (7%)
  starting transfers between devices  9.82 us (5%)
  other arithmetic  4.44 us (2%)
  local copies, waits for them, and re-layouts  2.49 us (1%)
    reduce_scatter x1, waiting for transfers between devices, local(): lax.psum_scatter(grad_term.astype(jnp.bfloat16), 'section', scatter_dimen...  25.8 us
    all_to_all x1, blocking collectives, local(): lax.all_to_all(sent_rows, 'expert', split_axis=0, concat_axis=0, tiled=True)  25.3 us
    reduce_scatter x1, waiting for transfers between devices, local(): lax.psum_scatter(up_term.astype(jnp.bfloat16), 'section', scatter_dimensi...  21.7 us
    all_to_all x1, blocking collectives, local(): lax.all_to_all(sent_grads, 'expert', split_axis=0, concat_axis=0, tiled=T...  21.3 us
    all_to_all x1, waiting for transfers between devices, local(): lax.all_to_all(out_rows, 'expert', split_axis=0, concat_axis=0, tiled=True)  13.2 us
    all_gather x1, blocking collectives, local(): lax.all_gather(gate_grad, 'section', axis=1, tiled=True)  8.71 us
    all_gather x1, blocking collectives, local(): lax.all_gather(hidden, 'section', axis=1, tiled=True)  8.62 us
    all_gather x1, blocking collectives, local(): lax.all_gather(up_grad, 'section', axis=1, tiled=True)  8.01 us
  transfers between devices with their start and end apart: 5, of which 4 were waited for; matrix products, arithmetic and copies ran while one was open for 7% of the time, Pallas kernels for 0%

commit v1 on v0

--- a/solution.py
+++ b/solution.py
@@ -1,6 +1,10 @@
+import functools
+
 import jax
 import jax.numpy as jnp
 from jax import lax
+from jax.experimental import pallas as pl
+from jax.experimental.pallas import tpu as pltpu
 from jax.sharding import PartitionSpec as P
 
 
@@ -8,7 +12,7 @@
     tok_rows, top_count = expert_ids.shape
     col_span = tokens.shape[1]
     expert_count = lax.axis_size("expert")
-    capacity = min(tok_rows, max(2, 3 * tok_rows * top_count // (2 * expert_count)))
+    capacity = capacity_of(tok_rows, top_count, expert_count)
     slot_total = expert_count * capacity
     one_hot = (
         expert_ids[:, :, None] == jnp.arange(expert_count, dtype=jnp.int32)[None, None, :]
@@ -83,6 +87,322 @@
     return (mixed, token_grads, down_grad[None])
 
 
+MESH = pl.DeviceIdType.MESH
+GROUPS = 4
+ORDER = (0, 2, 1, 3)
+NT = (((1,), (1,)), ((), ()))
+TN = (((0,), (0,)), ((), ()))
+F32 = jnp.float32
+BF = jnp.bfloat16
+
+
+def expert_kernel(
+    n_exp, cap, ids_c, ids_r, gate_c, gate_r, tok, cot, wg_h, wu_h, wd_h,
+    mixed_o, tgrad_o, dg_o,
+    wg, wu, wd, send, recv, part, r1, s2, r2, act, hbuf, obuf, back, dgbuf,
+    w_sem, d_ss, d_rs, s1_ss, s1_rs, s2_ss, s2_rs, gy_ss, gy_rs, gm_ss, gm_rs,
+    gr_ss, gr_rs, b_ss, b_rs, loc_sem, o_sem,
+):
+    me_e = lax.axis_index("expert")
+    me_s = lax.axis_index("section")
+    span = n_exp // GROUPS
+    my_g, my_x = me_e // span, me_e % span
+    my_y, my_c = me_s // 2, me_s % 2
+    oth_y, oth_c = 1 - my_y, 1 - my_c
+    mate = my_y * 2 + oth_c
+    ypart = oth_y * 2 + my_c
+    rows = span * cap
+    slots = n_exp * cap
+    n_tok, cols = tok.shape
+    quarter = part.shape[-1]
+    topk = ids_c.shape[1]
+
+    def group_of(c):
+        return ((my_g // 2 + c // 2) % 2) * 2 + (my_g % 2 + c % 2) % 2
+
+    def peers(c):
+        return [group_of(c) * span + (my_x + i) % span for i in range(span)]
+
+    loads = [
+        pltpu.make_async_copy(a, b, w_sem.at[i])
+        for i, (a, b) in enumerate(((wg_h, wg), (wu_h, wu), (wd_h, wd)))
+    ]
+    for load in loads:
+        load.start()
+
+    barrier = pltpu.get_barrier_semaphore()
+    for i in range(1, n_exp):
+        pl.semaphore_signal(
+            barrier, inc=1, device_id=(me_s, (me_e + i) % n_exp), device_id_type=MESH
+        )
+    for s in (mate, ypart):
+        pl.semaphore_signal(barrier, inc=1, device_id=(s, me_e), device_id_type=MESH)
+
+    e_r = lax.broadcasted_iota(jnp.int32, (n_exp, n_tok), 0)
+    hot_r = [(ids_r[k : k + 1, :] == e_r).astype(F32) for k in range(topk)]
+    t0 = lax.broadcasted_iota(jnp.int32, (n_tok, n_tok), 0)
+    t1 = lax.broadcasted_iota(jnp.int32, (n_tok, n_tok), 1)
+    earlier_r = jnp.dot(
+        sum(hot_r).astype(BF), (t0 < t1).astype(BF), preferred_element_type=F32
+    )
+    s_iota = lax.broadcasted_iota(jnp.int32, (slots, n_tok), 0)
+    chooser = jnp.zeros((slots, n_tok), F32)
+    gcol = jnp.zeros((slots, 1), F32)
+    for k in range(topk):
+        base = earlier_r + sum(hot_r[:k], jnp.zeros_like(earlier_r))
+        slot_k = jnp.sum(hot_r[k] * (base + e_r.astype(F32) * cap), axis=0, keepdims=True)
+        hit = (slot_k.astype(jnp.int32) == s_iota).astype(F32)
+        chooser = chooser + hit
+        gcol = gcol + jnp.sum(hit * gate_r[k : k + 1, :], axis=1, keepdims=True)
+    chooser = chooser.astype(BF)
+    picked = jnp.dot(chooser, tok[...], preferred_element_type=F32).astype(BF)
+    send[:, 0] = picked.reshape(n_exp, cap, cols)
+    picked = (jnp.dot(chooser, cot[...], preferred_element_type=F32) * gcol).astype(BF)
+    send[:, 1] = picked.reshape(n_exp, cap, cols)
+
+    pl.semaphore_wait(barrier, n_exp + 1)
+
+    def dispatch(peer):
+        return pltpu.make_async_remote_copy(
+            src_ref=send.at[peer], dst_ref=recv.at[me_e], send_sem=d_ss.at[peer],
+            recv_sem=d_rs.at[me_e], device_id=(me_s, peer), device_id_type=MESH,
+        )
+
+    def arrived(peer):
+        return pltpu.make_async_remote_copy(
+            src_ref=send.at[peer], dst_ref=recv.at[peer], send_sem=d_ss.at[peer],
+            recv_sem=d_rs.at[peer], device_id=(me_s, peer), device_id_type=MESH,
+        )
+
+    def give(peer):
+        return pltpu.make_async_remote_copy(
+            src_ref=obuf.at[peer], dst_ref=back.at[me_e], send_sem=b_ss.at[peer],
+            recv_sem=b_rs.at[me_e], device_id=(me_s, peer), device_id_type=MESH,
+        )
+
+    def given(peer):
+        return pltpu.make_async_remote_copy(
+            src_ref=obuf.at[peer], dst_ref=back.at[peer], send_sem=b_ss.at[peer],
+            recv_sem=b_rs.at[peer], device_id=(me_s, peer), device_id_type=MESH,
+        )
+
+    def to_section(src, dst, ss, rs, s):
+        return pltpu.make_async_remote_copy(
+            src_ref=src, dst_ref=dst, send_sem=ss, recv_sem=rs,
+            device_id=(s, me_e), device_id_type=MESH,
+        )
+
+    own = pltpu.make_async_copy(send.at[me_e], recv.at[me_e], loc_sem.at[0])
+    own.start()
+    for c in ORDER:
+        for i, peer in enumerate(peers(c)):
+            if c or i:
+                dispatch(peer).start()
+    for load in loads:
+        load.wait()
+
+    def rs1(c):
+        return to_section(part.at[c, oth_c], r1.at[c], s1_ss.at[c], s1_rs.at[c], mate)
+
+    def rs2(c):
+        return to_section(s2.at[c], r2.at[c], s2_ss.at[c], s2_rs.at[c], ypart)
+
+    def ag_y(c, y=None):
+        mine = act.at[c, my_c, my_y if y is None else y]
+        return to_section(mine, mine, gy_ss.at[c], gy_rs.at[c], ypart)
+
+    def ag_m(c, core=None):
+        mine = act.at[c, my_c if core is None else core, my_y]
+        return to_section(mine, mine, gm_ss.at[c], gm_rs.at[c], mate)
+
+    def ag_r(c, core=None):
+        mine = act.at[c, my_c if core is None else core, oth_y]
+        return to_section(mine, mine, gr_ss.at[c], gr_rs.at[c], mate)
+
+    def stage_a(c):
+        for i, peer in enumerate(peers(c)):
+            if c or i:
+                arrived(peer).wait_recv()
+            else:
+                own.wait()
+        first = group_of(c) * span
+        x = recv[pl.ds(first, span), 0].reshape(rows, cols)
+        g = recv[pl.ds(first, span), 1].reshape(rows, cols)
+        for q in range(4):
+            at = slice(q * quarter, (q + 1) * quarter)
+            part[c, q // 2, q % 2, 0] = jnp.dot(
+                x, wg[:, at], preferred_element_type=F32).astype(BF)
+            part[c, q // 2, q % 2, 1] = jnp.dot(
+                x, wu[:, at], preferred_element_type=F32).astype(BF)
+            part[c, q // 2, q % 2, 2] = lax.dot_general(
+                g, wd[at, :], NT, preferred_element_type=F32).astype(BF)
+        rs1(c).start()
+
+    def stage_b(c):
+        rs1(c).wait_recv()
+        s2[c] = (part[c, my_c, oth_y].astype(F32) + r1[c, oth_y].astype(F32)).astype(BF)
+        rs2(c).start()
+
+    def stage_c(c):
+        rs2(c).wait_recv()
+        total = (
+            part[c, my_c, my_y].astype(F32) + r1[c, my_y].astype(F32) + r2[c].astype(F32)
+        )
+        pre, up, hg = total[0], total[1], total[2]
+        sig = jax.nn.sigmoid(pre)
+        silu = pre * sig
+        act[c, my_c, my_y, 0] = (silu * up).astype(BF)
+        act[c, my_c, my_y, 1] = (hg * up * sig * (1.0 + pre * (1.0 - sig))).astype(BF)
+        act[c, my_c, my_y, 2] = (hg * silu).astype(BF)
+        ag_y(c).start()
+        ag_m(c).start()
+
+    def stage_d(c):
+        ag_y(c, oth_y).wait_recv()
+        ag_r(c).start()
+
+    def stage_e(c):
+        ag_m(c, oth_c).wait_recv()
+        ag_r(c, oth_c).wait_recv()
+        h, gg, ug = [
+            jnp.concatenate([act[c, q // 2, q % 2, j] for q in range(4)], axis=1)
+            for j in range(3)
+        ]
+        group = group_of(c)
+        hbuf[group] = h
+        first = group * span
+        out = jnp.dot(h, wd[...], preferred_element_type=F32).astype(BF)
+        obuf[pl.ds(first, span), 0] = out.reshape(span, cap, cols)
+        sg = lax.dot_general(gg, wg[...], NT, preferred_element_type=F32)
+        sg = (sg + lax.dot_general(ug, wu[...], NT, preferred_element_type=F32)).astype(BF)
+        obuf[pl.ds(first, span), 1] = sg.reshape(span, cap, cols)
+        for i, peer in enumerate(peers(c)):
+            if c or i:
+                give(peer).start()
+            else:
+                pltpu.make_async_copy(obuf.at[me_e], back.at[me_e], loc_sem.at[1]).start()
+
+    c0, c1, c2, c3 = ORDER
+    for stage, c in (
+        (stage_a, c0), (stage_b, c0), (stage_c, c0), (stage_d, c0), (stage_e, c0),
+        (stage_a, c1), (stage_b, c1), (stage_a, c2), (stage_c, c1), (stage_b, c2),
+        (stage_d, c1), (stage_c, c2), (stage_e, c1), (stage_d, c2), (stage_a, c3),
+        (stage_e, c2), (stage_b, c3), (stage_c, c3), (stage_d, c3), (stage_e, c3),
+    ):
+        stage(c)
+
+    store = pltpu.make_async_copy(dgbuf, dg_o, o_sem)
+    all_g = recv[:, 1].reshape(slots, cols)
+    for q in range(4):
+        at = slice(q * quarter, (q + 1) * quarter)
+        hq = hbuf[:, :, at].reshape(slots, quarter)
+        dgbuf[at, :] = lax.dot_general(hq, all_g, TN, preferred_element_type=F32).astype(BF)
+    store.start()
+
+    e_c = lax.broadcasted_iota(jnp.int32, (n_tok, n_exp), 1)
+    hot_c = [(ids_c[:, k : k + 1] == e_c).astype(F32) for k in range(topk)]
+    earlier_c = jnp.dot((t1 < t0).astype(BF), sum(hot_c).astype(BF), preferred_element_type=F32)
+    l_iota = lax.broadcasted_iota(jnp.int32, (n_tok, slots), 1)
+    picks = []
+    for k in range(topk):
+        base = earlier_c + sum(hot_c[:k], jnp.zeros_like(earlier_c))
+        slot_k = jnp.sum(hot_c[k] * (base + e_c.astype(F32) * cap), axis=1, keepdims=True)
+        picks.append((slot_k.astype(jnp.int32) == l_iota).astype(F32))
+
+    for c in ORDER:
+        for i, peer in enumerate(peers(c)):
+            if c or i:
+                given(peer).wait_recv()
+            else:
+                pltpu.make_async_copy(obuf.at[me_e], back.at[me_e], loc_sem.at[1]).wait()
+    outs = back[:, 0].reshape(slots, cols)
+    mixed = sum(
+        gate_c[:, k : k + 1]
+        * jnp.dot(picks[k].astype(BF), outs, preferred_element_type=F32)
+        for k in range(topk)
+    )
+    mixed_o[...] = mixed.astype(BF)
+    tgrad_o[...] = jnp.dot(
+        sum(picks).astype(BF), back[:, 1].reshape(slots, cols), preferred_element_type=F32
+    ).astype(BF)
+
+    for c in ORDER:
+        for i, peer in enumerate(peers(c)):
+            if c or i:
+                dispatch(peer).wait_send()
+                give(peer).wait_send()
+        for copy in (rs1(c), rs2(c), ag_y(c), ag_m(c), ag_r(c)):
+            copy.wait_send()
+    store.wait()
+
+
+def fused(tokens, expert_ids, gates, cotangent, w_gate, w_up, w_down):
+    n_tok, topk = expert_ids.shape
+    cols = tokens.shape[1]
+    hid = w_gate.shape[2]
+    n_exp, n_sec = lax.axis_size("expert"), lax.axis_size("section")
+    cap = capacity_of(n_tok, topk, n_exp)
+    rows = n_exp // GROUPS * cap
+    quarter = hid // n_sec
+    vm = pl.BlockSpec(memory_space=pltpu.VMEM)
+    hbm = pl.BlockSpec(memory_space=pl.ANY)
+    dma = pltpu.SemaphoreType.DMA
+    per = (GROUPS, 2, 2, 3, rows, quarter)
+    mixed, tgrad, dg = pl.pallas_call(
+        functools.partial(expert_kernel, n_exp, cap),
+        out_shape=(
+            jax.ShapeDtypeStruct((n_tok, cols), BF),
+            jax.ShapeDtypeStruct((n_tok, cols), BF),
+            jax.ShapeDtypeStruct((hid, cols), BF),
+        ),
+        in_specs=[vm] * 6 + [hbm] * 3,
+        out_specs=(vm, vm, hbm),
+        scratch_shapes=[
+            pltpu.VMEM((cols, hid), BF),
+            pltpu.VMEM((cols, hid), BF),
+            pltpu.VMEM((hid, cols), BF),
+            pltpu.VMEM((n_exp, 2, cap, cols), BF),
+            pltpu.VMEM((n_exp, 2, cap, cols), BF),
+            pltpu.VMEM(per, BF),
+            pltpu.VMEM((GROUPS, 2, 3, rows, quarter), BF),
+            pltpu.VMEM((GROUPS, 3, rows, quarter), BF),
+            pltpu.VMEM((GROUPS, 3, rows, quarter), BF),
+            pltpu.VMEM(per, BF),
+            pltpu.VMEM((GROUPS, rows, hid), BF),
+            pltpu.VMEM((n_exp, 2, cap, cols), BF),
+            pltpu.VMEM((n_exp, 2, cap, cols), BF),
+            pltpu.VMEM((hid, cols), BF),
+            dma((3,)),
+            dma((n_exp,)), dma((n_exp,)),
+        ]
+        + [dma((GROUPS,)) for _ in range(10)]
+        + [dma((n_exp,)), dma((n_exp,)), dma((2,)), dma],
+        compiler_params=pltpu.CompilerParams(
+            collective_id=0, has_side_effects=True, vmem_limit_bytes=60 * 1024 * 1024
+        ),
+    )(
+        expert_ids, expert_ids.T, gates, gates.T, tokens, cotangent,
+        w_gate[0], w_up[0], w_down[0],
+    )
+    return mixed, tgrad, dg[None]
+
+
+def capacity_of(tok_rows, top_count, expert_count):
+    return min(tok_rows, max(2, 3 * tok_rows * top_count // (2 * expert_count)))
+
+
+def layer(tokens, expert_ids, *rest):
+    n_exp, n_sec = lax.axis_size("expert"), lax.axis_size("section")
+    n_tok, topk = expert_ids.shape
+    cap = capacity_of(n_tok, topk, n_exp)
+    hid = rest[2].shape[2]
+    tiles = (
+        n_exp % GROUPS == 0 and n_sec == 4 and cap % 16 == 0 and n_tok % 128 == 0
+        and tokens.shape[1] % 128 == 0 and hid % (n_sec * 128) == 0
+    )
+    return (fused if tiles else local)(tokens, expert_ids, *rest)
+
+
 def solution(mesh):
     placed = (
         P("expert", "section"),
@@ -94,7 +414,7 @@
         P("expert", None, "section"),
     )
     return jax.shard_map(
-        local,
+        layer,
         mesh=mesh,
         in_specs=placed,
         out_specs=(P("expert", "section"), P("expert", "section"), P("expert", None, "section")),

time: 191 us -> 90.1 us (0.47)
  the two profiles are of different devices: /device:TPU:0 before, /device:TPU:17 now
where the time goes in v1:
time: 90.1 us; the launch traced here: 89.9 us
  Pallas kernels  80.3 us (89%)
  local copies, waits for them, and re-layouts  8.99 us (10%)
    pallas_call x1, Pallas kernels, fused(): pl.pallas_call(functools.partial(expert_kernel, n_exp, cap), out_shape=(j...  80.3 us
    unnamed x5, local copies, waits for them, and re-layouts  8.99 us

profile of v1, /device:TPU:17, one launch (start us, length us, event | category | flops | bytes accessed | tf_op | source)
XLA Modules:
  0.0 89.9 jit_solution(14541007906015462267)
XLA Ops:
  0.6 1.4 %copy.10.ids_c = s32[128,2]{1,0:T(8,128)} copy(s32[128,2]{0,1:T(2,128)} %param.8) | data formatting | bytes 2048 | tf_op args[1]
  2.0 1.4 %copy.11.gate_c = f32[128,2]{1,0:T(8,128)} copy(f32[128,2]{0,1:T(2,128)} %param.9) | data formatting | bytes 2048 | tf_op args[2]
  3.5 80.3 %shard_map.94 = (bf16[128,896]{1,0:T(8,128)(2,1)}, bf16[128,896]{1,0:T(8,128)(2,1)}, bf16[1024,896]{1,0:T(8,128)(2,1)}) custom-call(s32[128,2]{1,0:T(8,128)} %copy.10.ids_c, s32[2,128]{1,0:T(2,128)} %bitcast.10, f32[128,2]{1,0:T(8,128)} %copy.11.gate_c, f32[2,128]{1,0:T(2,128)} %bitcast.11, bf16[128,896]{1,0:T(8,128)(2,1)} %tok.1, bf16[128,896]{1,0:T(8,128)(2,1)} %cot.1, ...), custom_call_target="tpu_custom_call" | custom-call | tf_op jit(solution)/shard_map/pallas_call | solution.py:351
  83.7 1.6 %copy.15 = bf16[128,896]{1,0:T(8,128)(2,1)} copy(bf16[128,896]{1,0:T(8,128)(2,1)} %get-tuple-element.12) | data formatting | bytes 458752
  85.4 1.6 %copy.16 = bf16[128,896]{1,0:T(8,128)(2,1)} copy(bf16[128,896]{1,0:T(8,128)(2,1)} %get-tuple-element.13) | data formatting | bytes 458752
  87.0 2.9 %copy.17 = bf16[1,1024,896]{2,1,0:T(8,128)(2,1)} copy(bf16[1,1024,896]{2,1,0:T(8,128)(2,1)} %bitcast.6) | data formatting | bytes 3670016

commit v2 on v1

--- a/solution.py
+++ b/solution.py
@@ -90,6 +90,7 @@
 MESH = pl.DeviceIdType.MESH
 GROUPS = 4
 ORDER = (0, 2, 1, 3)
+DISPATCH = (2, 0, 1, 3)
 NT = (((1,), (1,)), ((), ()))
 TN = (((0,), (0,)), ((), ()))
 F32 = jnp.float32
@@ -97,9 +98,9 @@
 
 
 def expert_kernel(
-    n_exp, cap, ids_c, ids_r, gate_c, gate_r, tok, cot, wg_h, wu_h, wd_h,
-    mixed_o, tgrad_o, dg_o,
-    wg, wu, wd, send, recv, part, r1, s2, r2, act, hbuf, obuf, back, dgbuf,
+    n_exp, cap, ids_r, gate_r, tok, cot, wg_h, wu_h, wd_h,
+    back, dg_o,
+    wg, wu, wd, send, recv, part, r1, s2, r2, act, hbuf, obuf, dgbuf,
     w_sem, d_ss, d_rs, s1_ss, s1_rs, s2_ss, s2_rs, gy_ss, gy_rs, gm_ss, gm_rs,
     gr_ss, gr_rs, b_ss, b_rs, loc_sem, o_sem,
 ):
@@ -115,7 +116,7 @@
     slots = n_exp * cap
     n_tok, cols = tok.shape
     quarter = part.shape[-1]
-    topk = ids_c.shape[1]
+    topk = ids_r.shape[0]
 
     def group_of(c):
         return ((my_g // 2 + c // 2) % 2) * 2 + (my_g % 2 + c % 2) % 2
@@ -145,23 +146,6 @@
     earlier_r = jnp.dot(
         sum(hot_r).astype(BF), (t0 < t1).astype(BF), preferred_element_type=F32
     )
-    s_iota = lax.broadcasted_iota(jnp.int32, (slots, n_tok), 0)
-    chooser = jnp.zeros((slots, n_tok), F32)
-    gcol = jnp.zeros((slots, 1), F32)
-    for k in range(topk):
-        base = earlier_r + sum(hot_r[:k], jnp.zeros_like(earlier_r))
-        slot_k = jnp.sum(hot_r[k] * (base + e_r.astype(F32) * cap), axis=0, keepdims=True)
-        hit = (slot_k.astype(jnp.int32) == s_iota).astype(F32)
-        chooser = chooser + hit
-        gcol = gcol + jnp.sum(hit * gate_r[k : k + 1, :], axis=1, keepdims=True)
-    chooser = chooser.astype(BF)
-    picked = jnp.dot(chooser, tok[...], preferred_element_type=F32).astype(BF)
-    send[:, 0] = picked.reshape(n_exp, cap, cols)
-    picked = (jnp.dot(chooser, cot[...], preferred_element_type=F32) * gcol).astype(BF)
-    send[:, 1] = picked.reshape(n_exp, cap, cols)
-
-    pl.semaphore_wait(barrier, n_exp + 1)
-
     def dispatch(peer):
         return pltpu.make_async_remote_copy(
             src_ref=send.at[peer], dst_ref=recv.at[me_e], send_sem=d_ss.at[peer],
@@ -192,12 +176,33 @@
             device_id=(s, me_e), device_id_type=MESH,
         )
 
+    slot_r = []
+    for k in range(topk):
+        base = earlier_r + sum(hot_r[:k], jnp.zeros_like(earlier_r))
+        slot_k = jnp.sum(hot_r[k] * (base + e_r.astype(F32) * cap), axis=0, keepdims=True)
+        slot_r.append(slot_k.astype(jnp.int32))
+    s_iota = lax.broadcasted_iota(jnp.int32, (rows, n_tok), 0)
     own = pltpu.make_async_copy(send.at[me_e], recv.at[me_e], loc_sem.at[0])
-    own.start()
-    for c in ORDER:
+    for c in DISPATCH:
+        first = group_of(c) * span
+        chooser = jnp.zeros((rows, n_tok), F32)
+        gcol = jnp.zeros((rows, 1), F32)
+        for k in range(topk):
+            hit = (slot_r[k] - first * cap == s_iota).astype(F32)
+            chooser = chooser + hit
+            gcol = gcol + jnp.sum(hit * gate_r[k : k + 1, :], axis=1, keepdims=True)
+        chooser = chooser.astype(BF)
+        picked = jnp.dot(chooser, tok[...], preferred_element_type=F32).astype(BF)
+        send[pl.ds(first, span), 0] = picked.reshape(span, cap, cols)
+        picked = (jnp.dot(chooser, cot[...], preferred_element_type=F32) * gcol).astype(BF)
+        send[pl.ds(first, span), 1] = picked.reshape(span, cap, cols)
+        if c == DISPATCH[0]:
+            pl.semaphore_wait(barrier, n_exp + 1)
         for i, peer in enumerate(peers(c)):
             if c or i:
                 dispatch(peer).start()
+            else:
+                own.start()
     for load in loads:
         load.wait()
 
@@ -285,9 +290,9 @@
     c0, c1, c2, c3 = ORDER
     for stage, c in (
         (stage_a, c0), (stage_b, c0), (stage_c, c0), (stage_d, c0), (stage_e, c0),
-        (stage_a, c1), (stage_b, c1), (stage_a, c2), (stage_c, c1), (stage_b, c2),
-        (stage_d, c1), (stage_c, c2), (stage_e, c1), (stage_d, c2), (stage_a, c3),
-        (stage_e, c2), (stage_b, c3), (stage_c, c3), (stage_d, c3), (stage_e, c3),
+        (stage_a, c1), (stage_b, c1), (stage_c, c1), (stage_d, c1), (stage_e, c1),
+        (stage_a, c2), (stage_b, c2), (stage_a, c3), (stage_c, c2), (stage_b, c3),
+        (stage_d, c2), (stage_c, c3), (stage_e, c2), (stage_d, c3), (stage_e, c3),
     ):
         stage(c)
 
@@ -299,33 +304,12 @@
         dgbuf[at, :] = lax.dot_general(hq, all_g, TN, preferred_element_type=F32).astype(BF)
     store.start()
 
-    e_c = lax.broadcasted_iota(jnp.int32, (n_tok, n_exp), 1)
-    hot_c = [(ids_c[:, k : k + 1] == e_c).astype(F32) for k in range(topk)]
-    earlier_c = jnp.dot((t1 < t0).astype(BF), sum(hot_c).astype(BF), preferred_element_type=F32)
-    l_iota = lax.broadcasted_iota(jnp.int32, (n_tok, slots), 1)
-    picks = []
-    for k in range(topk):
-        base = earlier_c + sum(hot_c[:k], jnp.zeros_like(earlier_c))
-        slot_k = jnp.sum(hot_c[k] * (base + e_c.astype(F32) * cap), axis=1, keepdims=True)
-        picks.append((slot_k.astype(jnp.int32) == l_iota).astype(F32))
-
     for c in ORDER:
         for i, peer in enumerate(peers(c)):
             if c or i:
                 given(peer).wait_recv()
             else:
                 pltpu.make_async_copy(obuf.at[me_e], back.at[me_e], loc_sem.at[1]).wait()
-    outs = back[:, 0].reshape(slots, cols)
-    mixed = sum(
-        gate_c[:, k : k + 1]
-        * jnp.dot(picks[k].astype(BF), outs, preferred_element_type=F32)
-        for k in range(topk)
-    )
-    mixed_o[...] = mixed.astype(BF)
-    tgrad_o[...] = jnp.dot(
-        sum(picks).astype(BF), back[:, 1].reshape(slots, cols), preferred_element_type=F32
-    ).astype(BF)
-
     for c in ORDER:
         for i, peer in enumerate(peers(c)):
             if c or i:
@@ -334,6 +318,64 @@
         for copy in (rs1(c), rs2(c), ag_y(c), ag_m(c), ag_r(c)):
             copy.wait_send()
     store.wait()
+
+
+def combine_kernel(n_exp, cap, ids_r, gate_r, back_h, dg_h, mixed_o, tgrad_o, dg_o, back, dg, sem):
+    topk, n_tok = ids_r.shape
+    hid, cols = dg.shape
+    slots = n_exp * cap
+    part = hid // GROUPS
+    half = n_exp // 2
+    gets = [
+        pltpu.make_async_copy(
+            back_h.at[pl.ds(i * half, half)], back.at[pl.ds(i * half, half)], sem.at[i]
+        )
+        for i in range(2)
+    ]
+    ins = [
+        pltpu.make_async_copy(
+            dg_h.at[pl.ds(i * part, part)], dg.at[pl.ds(i * part, part)], sem.at[2 + i]
+        )
+        for i in range(GROUPS)
+    ]
+    outs = [
+        pltpu.make_async_copy(
+            dg.at[pl.ds(i * part, part)], dg_o.at[pl.ds(i * part, part)], sem.at[2 + GROUPS + i]
+        )
+        for i in range(GROUPS)
+    ]
+    for get in gets + ins:
+        get.start()
+    t0 = lax.broadcasted_iota(jnp.int32, (n_tok, n_tok), 0)
+    t1 = lax.broadcasted_iota(jnp.int32, (n_tok, n_tok), 1)
+    eye = (t0 == t1).astype(F32)
+    e_r = lax.broadcasted_iota(jnp.int32, (n_exp, n_tok), 0)
+    hot = [(ids_r[k : k + 1, :] == e_r).astype(F32) for k in range(topk)]
+    earlier = jnp.dot(sum(hot).astype(BF), (t0 < t1).astype(BF), preferred_element_type=F32)
+    l_iota = lax.broadcasted_iota(jnp.int32, (n_tok, slots), 1)
+    picks, weights = [], []
+    for k in range(topk):
+        base = earlier + sum(hot[:k], jnp.zeros_like(earlier))
+        slot_k = jnp.sum(hot[k] * (base + e_r.astype(F32) * cap), axis=0, keepdims=True)
+        column = jnp.sum(eye * slot_k, axis=1, keepdims=True).astype(jnp.int32)
+        picks.append((column == l_iota).astype(F32))
+        weights.append(jnp.sum(eye * gate_r[k : k + 1, :], axis=1, keepdims=True))
+    for get in gets:
+        get.wait()
+    for i in range(GROUPS):
+        ins[i].wait()
+        outs[i].start()
+    rows_out = back[:, 0].reshape(slots, cols)
+    mixed = sum(
+        weights[k] * jnp.dot(picks[k].astype(BF), rows_out, preferred_element_type=F32)
+        for k in range(topk)
+    )
+    mixed_o[...] = mixed.astype(BF)
+    tgrad_o[...] = jnp.dot(
+        sum(picks).astype(BF), back[:, 1].reshape(slots, cols), preferred_element_type=F32
+    ).astype(BF)
+    for put in outs:
+        put.wait()
 
 
 def fused(tokens, expert_ids, gates, cotangent, w_gate, w_up, w_down):
@@ -348,15 +390,15 @@
     hbm = pl.BlockSpec(memory_space=pl.ANY)
     dma = pltpu.SemaphoreType.DMA
     per = (GROUPS, 2, 2, 3, rows, quarter)
-    mixed, tgrad, dg = pl.pallas_call(
+    ids_r, gate_r = expert_ids.T, gates.T
+    back, dg = pl.pallas_call(
         functools.partial(expert_kernel, n_exp, cap),
         out_shape=(
-            jax.ShapeDtypeStruct((n_tok, cols), BF),
-            jax.ShapeDtypeStruct((n_tok, cols), BF),
+            jax.ShapeDtypeStruct((n_exp, 2, cap, cols), BF),
             jax.ShapeDtypeStruct((hid, cols), BF),
         ),
-        in_specs=[vm] * 6 + [hbm] * 3,
-        out_specs=(vm, vm, hbm),
+        in_specs=[vm] * 4 + [hbm] * 3,
+        out_specs=(hbm, hbm),
         scratch_shapes=[
             pltpu.VMEM((cols, hid), BF),
             pltpu.VMEM((cols, hid), BF),
@@ -370,7 +412,6 @@
             pltpu.VMEM(per, BF),
             pltpu.VMEM((GROUPS, rows, hid), BF),
             pltpu.VMEM((n_exp, 2, cap, cols), BF),
-            pltpu.VMEM((n_exp, 2, cap, cols), BF),
             pltpu.VMEM((hid, cols), BF),
             dma((3,)),
             dma((n_exp,)), dma((n_exp,)),
@@ -380,10 +421,23 @@
         compiler_params=pltpu.CompilerParams(
             collective_id=0, has_side_effects=True, vmem_limit_bytes=60 * 1024 * 1024
         ),
-    )(
-        expert_ids, expert_ids.T, gates, gates.T, tokens, cotangent,
-        w_gate[0], w_up[0], w_down[0],
-    )
+    )(ids_r, gate_r, tokens, cotangent, w_gate[0], w_up[0], w_down[0])
+    mixed, tgrad, dg = pl.pallas_call(
+        functools.partial(combine_kernel, n_exp, cap),
+        out_shape=(
+            jax.ShapeDtypeStruct((n_tok, cols), BF),
+            jax.ShapeDtypeStruct((n_tok, cols), BF),
+            jax.ShapeDtypeStruct((hid, cols), BF),
+        ),
+        in_specs=[vm] * 2 + [hbm] * 2,
+        out_specs=(vm, vm, hbm),
+        scratch_shapes=[
+            pltpu.VMEM((n_exp, 2, cap, cols), BF),
+            pltpu.VMEM((hid, cols), BF),
+            dma((2 + 2 * GROUPS,)),
+        ],
+        compiler_params=pltpu.CompilerParams(vmem_limit_bytes=32 * 1024 * 1024),
+    )(ids_r, gate_r, back, dg)
     return mixed, tgrad, dg[None]
 
 

time: 90.1 us -> 88.7 us (0.984)
  the two profiles are of different devices: /device:TPU:17 before, /device:TPU:21 now
where the time goes in v2:
time: 88.7 us; the launch traced here: 88.5 us
  Pallas kernels  85 us (96%)
  local copies, waits for them, and re-layouts  2.84 us (3%)
    pallas_call x1, Pallas kernels, fused(): pl.pallas_call(functools.partial(expert_kernel, n_exp, cap), out_shape=(j...  81.1 us
    pallas_call x1, Pallas kernels, fused(): pl.pallas_call(functools.partial(combine_kernel, n_exp, cap), out_shape=(...  3.92 us
    unnamed x8, local copies, waits for them, and re-layouts  2.84 us

profile of v2, /device:TPU:21, one launch (start us, length us, event | category | flops | bytes accessed | tf_op | source)
XLA Modules:
  0.0 88.5 jit_solution(10417680260129126310)
XLA Ops:
  0.6 0.0 copy-start.2
  0.6 0.0 copy-start.3
  0.7 81.1 %shard_map.94 = (bf16[8,2,48,896]{3,2,1,0:T(8,128)(2,1)}, bf16[1024,896]{1,0:T(8,128)(2,1)}) custom-call(s32[2,128]{1,0:T(2,128)} %bitcast.6, f32[2,128]{1,0:T(2,128)} %bitcast.8, bf16[128,896]{1,0:T(8,128)(2,1)} %tok.1, bf16[128,896]{1,0:T(8,128)(2,1)} %cot.1, bf16[896,1024]{1,0:T(8,128)(2,1)} %bitcast.10, bf16[896,1024]{1,0:T(8,128)(2,1)} %bitcast.11, ...), custom_call_target="tpu_custom_call" | custom-call | tf_op jit(solution)/shard_map/pallas_call | solution.py:394
  81.7 0.0 copy-done.2
  81.7 0.0 copy-done.3
  81.7 0.0 copy-start
  81.8 1.5 %copy-done = bf16[1024,896]{1,0:T(8,128)(2,1)S(1)} copy-done((bf16[1024,896]{1,0:T(8,128)(2,1)S(1)}, bf16[1024,896]{1,0:T(8,128)(2,1)}, u32[]{:S(2)}) %copy-start) | copy-done | bytes 1835032
  83.2 0.0 copy-start.1
  83.2 1.3 %copy-done.1 = bf16[8,2,48,896]{3,2,1,0:T(8,128)(2,1)S(1)} copy-done((bf16[8,2,48,896]{3,2,1,0:T(8,128)(2,1)S(1)}, bf16[8,2,48,896]{3,2,1,0:T(8,128)(2,1)}, u32[]{:S(2)}) %copy-start.1) | copy-done | bytes 1376280
  84.6 3.9 %shard_map.95 = (bf16[128,896]{1,0:T(8,128)(2,1)}, bf16[128,896]{1,0:T(8,128)(2,1)}, bf16[1024,896]{1,0:T(8,128)(2,1)}) custom-call(s32[2,128]{1,0:T(2,128)S(1)} %bitcast.7, f32[2,128]{1,0:T(2,128)S(1)} %bitcast.9, bf16[8,2,48,896]{3,2,1,0:T(8,128)(2,1)S(1)} %copy-done.1, bf16[1024,896]{1,0:T(8,128)(2,1)S(1)} %copy-done), custom_call_target="tpu_custom_call" | custom-call | tf_op jit(solution)/shard_map/pallas_call | solution.py:425
Async XLA Ops:
  0.6 81.1 %copy-start.2 = (s32[128,2]{0,1:T(2,128)S(1)}, s32[128,2]{0,1:T(2,128)}, u32[]{:S(2)}) copy-start(s32[128,2]{0,1:T(2,128)} %param.8) | copy-start | bytes 3076
  0.6 81.1 %copy-start.3 = (f32[128,2]{0,1:T(2,128)S(1)}, f32[128,2]{0,1:T(2,128)}, u32[]{:S(2)}) copy-start(f32[128,2]{0,1:T(2,128)} %param.9) | copy-start | bytes 3076
  81.7 1.5 %copy-start = (bf16[1024,896]{1,0:T(8,128)(2,1)S(1)}, bf16[1024,896]{1,0:T(8,128)(2,1)}, u32[]{:S(2)}) copy-start(bf16[1024,896]{1,0:T(8,128)(2,1)} %get-tuple-element.9.dg_h) | copy-start | bytes 5505028
  83.2 1.3 %copy-start.1 = (bf16[8,2,48,896]{3,2,1,0:T(8,128)(2,1)S(1)}, bf16[8,2,48,896]{3,2,1,0:T(8,128)(2,1)}, u32[]{:S(2)}) copy-start(bf16[8,2,48,896]{3,2,1,0:T(8,128)(2,1)} %get-tuple-element.8.back_h) | copy-start | bytes 4128772

commit v3 on v2

--- a/solution.py
+++ b/solution.py
@@ -91,6 +91,11 @@
 GROUPS = 4
 ORDER = (0, 2, 1, 3)
 DISPATCH = (2, 0, 1, 3)
+STEPS = (
+    "A0", "B0", "A2", "B2", "C0", "C2", "A3", "D0", "B3", "D2",
+    "E2", "E0", "C3", "A1", "D3", "A4", "B1", "E3", "B4", "A5",
+    "C4", "B5", "C1", "D4", "C5", "E4", "D1", "D5", "E1", "E5",
+)
 NT = (((1,), (1,)), ((), ()))
 TN = (((0,), (0,)), ((), ()))
 F32 = jnp.float32
@@ -206,95 +211,132 @@
     for load in loads:
         load.wait()
 
-    def rs1(c):
-        return to_section(part.at[c, oth_c], r1.at[c], s1_ss.at[c], s1_rs.at[c], mate)
-
-    def rs2(c):
-        return to_section(s2.at[c], r2.at[c], s2_ss.at[c], s2_rs.at[c], ypart)
-
-    def ag_y(c, y=None):
-        mine = act.at[c, my_c, my_y if y is None else y]
-        return to_section(mine, mine, gy_ss.at[c], gy_rs.at[c], ypart)
-
-    def ag_m(c, core=None):
-        mine = act.at[c, my_c if core is None else core, my_y]
-        return to_section(mine, mine, gm_ss.at[c], gm_rs.at[c], mate)
-
-    def ag_r(c, core=None):
-        mine = act.at[c, my_c if core is None else core, oth_y]
-        return to_section(mine, mine, gr_ss.at[c], gr_rs.at[c], mate)
-
-    def stage_a(c):
-        for i, peer in enumerate(peers(c)):
-            if c or i:
+    def blocks(ch):
+        c, i, n = ch
+        return pl.ds(c * span + i, n)
+
+    def first_of(ch):
+        c, i, n = ch
+        return group_of(c) * span + (0 if n == span else (my_x + i) % span)
+
+    def members(ch):
+        c, i, n = ch
+        return [(c == 0 and j == 0, peers(c)[j]) for j in range(i, i + n)]
+
+    def sem_of(ch):
+        return ch[0] * span + ch[1]
+
+    def rs1(ch):
+        b, k = blocks(ch), sem_of(ch)
+        return to_section(part.at[b, oth_c], r1.at[b], s1_ss.at[k], s1_rs.at[k], mate)
+
+    def rs2(ch):
+        b, k = blocks(ch), sem_of(ch)
+        return to_section(s2.at[b], r2.at[b], s2_ss.at[k], s2_rs.at[k], ypart)
+
+    def ag_y(ch, y=None):
+        k = sem_of(ch)
+        mine = act.at[blocks(ch), my_c, my_y if y is None else y]
+        return to_section(mine, mine, gy_ss.at[k], gy_rs.at[k], ypart)
+
+    def ag_m(ch, core=None):
+        k = sem_of(ch)
+        mine = act.at[blocks(ch), my_c if core is None else core, my_y]
+        return to_section(mine, mine, gm_ss.at[k], gm_rs.at[k], mate)
+
+    def ag_r(ch, core=None):
+        k = sem_of(ch)
+        mine = act.at[blocks(ch), my_c if core is None else core, oth_y]
+        return to_section(mine, mine, gr_ss.at[k], gr_rs.at[k], mate)
+
+    def stage_a(ch):
+        n = ch[2]
+        for here, peer in members(ch):
+            if here:
+                own.wait()
+            else:
                 arrived(peer).wait_recv()
-            else:
-                own.wait()
-        first = group_of(c) * span
-        x = recv[pl.ds(first, span), 0].reshape(rows, cols)
-        g = recv[pl.ds(first, span), 1].reshape(rows, cols)
+        first = first_of(ch)
+        x = recv[pl.ds(first, n), 0].reshape(n * cap, cols)
+        g = recv[pl.ds(first, n), 1].reshape(n * cap, cols)
         for q in range(4):
             at = slice(q * quarter, (q + 1) * quarter)
-            part[c, q // 2, q % 2, 0] = jnp.dot(
-                x, wg[:, at], preferred_element_type=F32).astype(BF)
-            part[c, q // 2, q % 2, 1] = jnp.dot(
-                x, wu[:, at], preferred_element_type=F32).astype(BF)
-            part[c, q // 2, q % 2, 2] = lax.dot_general(
-                g, wd[at, :], NT, preferred_element_type=F32).astype(BF)
-        rs1(c).start()
-
-    def stage_b(c):
-        rs1(c).wait_recv()
-        s2[c] = (part[c, my_c, oth_y].astype(F32) + r1[c, oth_y].astype(F32)).astype(BF)
-        rs2(c).start()
-
-    def stage_c(c):
-        rs2(c).wait_recv()
-        total = (
-            part[c, my_c, my_y].astype(F32) + r1[c, my_y].astype(F32) + r2[c].astype(F32)
-        )
-        pre, up, hg = total[0], total[1], total[2]
+            terms = (
+                jnp.dot(x, wg[:, at], preferred_element_type=F32),
+                jnp.dot(x, wu[:, at], preferred_element_type=F32),
+                lax.dot_general(g, wd[at, :], NT, preferred_element_type=F32),
+            )
+            for j in range(3):
+                part[blocks(ch), q // 2, q % 2, j] = (
+                    terms[j].astype(BF).reshape(n, cap, quarter)
+                )
+        rs1(ch).start()
+
+    def stage_b(ch):
+        b = blocks(ch)
+        rs1(ch).wait_recv()
+        s2[b] = (part[b, my_c, oth_y].astype(F32) + r1[b, oth_y].astype(F32)).astype(BF)
+        rs2(ch).start()
+
+    def stage_c(ch):
+        b = blocks(ch)
+        rs2(ch).wait_recv()
+
+        def total(j):
+            return (
+                part[b, my_c, my_y, j].astype(F32) + r1[b, my_y, j].astype(F32)
+                + r2[b, j].astype(F32)
+            )
+
+        pre, up, hg = total(0), total(1), total(2)
         sig = jax.nn.sigmoid(pre)
         silu = pre * sig
-        act[c, my_c, my_y, 0] = (silu * up).astype(BF)
-        act[c, my_c, my_y, 1] = (hg * up * sig * (1.0 + pre * (1.0 - sig))).astype(BF)
-        act[c, my_c, my_y, 2] = (hg * silu).astype(BF)
-        ag_y(c).start()
-        ag_m(c).start()
-
-    def stage_d(c):
-        ag_y(c, oth_y).wait_recv()
-        ag_r(c).start()
-
-    def stage_e(c):
-        ag_m(c, oth_c).wait_recv()
-        ag_r(c, oth_c).wait_recv()
+        act[b, my_c, my_y, 0] = (silu * up).astype(BF)
+        act[b, my_c, my_y, 1] = (hg * up * sig * (1.0 + pre * (1.0 - sig))).astype(BF)
+        act[b, my_c, my_y, 2] = (hg * silu).astype(BF)
+        ag_y(ch).start()
+        ag_m(ch).start()
+
+    def stage_d(ch):
+        ag_y(ch, oth_y).wait_recv()
+        ag_r(ch).start()
+
+    def stage_e(ch):
+        n = ch[2]
+        ag_m(ch, oth_c).wait_recv()
+        ag_r(ch, oth_c).wait_recv()
         h, gg, ug = [
-            jnp.concatenate([act[c, q // 2, q % 2, j] for q in range(4)], axis=1)
+            jnp.concatenate(
+                [
+                    act[blocks(ch), q // 2, q % 2, j].reshape(n * cap, quarter)
+                    for q in range(4)
+                ],
+                axis=1,
+            )
             for j in range(3)
         ]
-        group = group_of(c)
-        hbuf[group] = h
-        first = group * span
+        first = first_of(ch)
+        hbuf[pl.ds(first, n)] = h.reshape(n, cap, 4 * quarter)
         out = jnp.dot(h, wd[...], preferred_element_type=F32).astype(BF)
-        obuf[pl.ds(first, span), 0] = out.reshape(span, cap, cols)
+        obuf[pl.ds(first, n), 0] = out.reshape(n, cap, cols)
         sg = lax.dot_general(gg, wg[...], NT, preferred_element_type=F32)
         sg = (sg + lax.dot_general(ug, wu[...], NT, preferred_element_type=F32)).astype(BF)
-        obuf[pl.ds(first, span), 1] = sg.reshape(span, cap, cols)
-        for i, peer in enumerate(peers(c)):
-            if c or i:
+        obuf[pl.ds(first, n), 1] = sg.reshape(n, cap, cols)
+        for here, peer in members(ch):
+            if here:
+                pltpu.make_async_copy(obuf.at[me_e], back.at[me_e], loc_sem.at[1]).start()
+            else:
                 give(peer).start()
-            else:
-                pltpu.make_async_copy(obuf.at[me_e], back.at[me_e], loc_sem.at[1]).start()
-
-    c0, c1, c2, c3 = ORDER
-    for stage, c in (
-        (stage_a, c0), (stage_b, c0), (stage_c, c0), (stage_d, c0), (stage_e, c0),
-        (stage_a, c1), (stage_b, c1), (stage_c, c1), (stage_d, c1), (stage_e, c1),
-        (stage_a, c2), (stage_b, c2), (stage_a, c3), (stage_c, c2), (stage_b, c3),
-        (stage_d, c2), (stage_c, c3), (stage_e, c2), (stage_d, c3), (stage_e, c3),
-    ):
-        stage(c)
+
+    stages = {"A": stage_a, "B": stage_b, "C": stage_c, "D": stage_d, "E": stage_e}
+    near = {"0": (0, 0, span), "1": (1, 0, span)}
+    half = span // 2
+    far = {
+        "2": (2, 0, half), "3": (2, half, half), "4": (3, 0, half), "5": (3, half, half)
+    }
+    chunks = {**near, **far}
+    for step in STEPS:
+        stages[step[0]](chunks[step[1]])
 
     store = pltpu.make_async_copy(dgbuf, dg_o, o_sem)
     all_g = recv[:, 1].reshape(slots, cols)
@@ -315,7 +357,8 @@
             if c or i:
                 dispatch(peer).wait_send()
                 give(peer).wait_send()
-        for copy in (rs1(c), rs2(c), ag_y(c), ag_m(c), ag_r(c)):
+    for ch in chunks.values():
+        for copy in (rs1(ch), rs2(ch), ag_y(ch), ag_m(ch), ag_r(ch)):
             copy.wait_send()
     store.wait()
 
@@ -384,12 +427,11 @@
     hid = w_gate.shape[2]
     n_exp, n_sec = lax.axis_size("expert"), lax.axis_size("section")
     cap = capacity_of(n_tok, topk, n_exp)
-    rows = n_exp // GROUPS * cap
     quarter = hid // n_sec
     vm = pl.BlockSpec(memory_space=pltpu.VMEM)
     hbm = pl.BlockSpec(memory_space=pl.ANY)
     dma = pltpu.SemaphoreType.DMA
-    per = (GROUPS, 2, 2, 3, rows, quarter)
+    per = (n_exp, 2, 2, 3, cap, quarter)
     ids_r, gate_r = expert_ids.T, gates.T
     back, dg = pl.pallas_call(
         functools.partial(expert_kernel, n_exp, cap),
@@ -406,17 +448,17 @@
             pltpu.VMEM((n_exp, 2, cap, cols), BF),
             pltpu.VMEM((n_exp, 2, cap, cols), BF),
             pltpu.VMEM(per, BF),
-            pltpu.VMEM((GROUPS, 2, 3, rows, quarter), BF),
-            pltpu.VMEM((GROUPS, 3, rows, quarter), BF),
-            pltpu.VMEM((GROUPS, 3, rows, quarter), BF),
+            pltpu.VMEM((n_exp, 2, 3, cap, quarter), BF),
+            pltpu.VMEM((n_exp, 3, cap, quarter), BF),
+            pltpu.VMEM((n_exp, 3, cap, quarter), BF),
             pltpu.VMEM(per, BF),
-            pltpu.VMEM((GROUPS, rows, hid), BF),
+            pltpu.VMEM((n_exp, cap, hid), BF),
             pltpu.VMEM((n_exp, 2, cap, cols), BF),
             pltpu.VMEM((hid, cols), BF),
             dma((3,)),
             dma((n_exp,)), dma((n_exp,)),
         ]
-        + [dma((GROUPS,)) for _ in range(10)]
+        + [dma((n_exp,)) for _ in range(10)]
         + [dma((n_exp,)), dma((n_exp,)), dma((2,)), dma],
         compiler_params=pltpu.CompilerParams(
             collective_id=0, has_side_effects=True, vmem_limit_bytes=60 * 1024 * 1024
@@ -436,7 +478,7 @@
             pltpu.VMEM((hid, cols), BF),
             dma((2 + 2 * GROUPS,)),
         ],
-        compiler_params=pltpu.CompilerParams(vmem_limit_bytes=32 * 1024 * 1024),
+        compiler_params=pltpu.CompilerParams(vmem_limit_bytes=60 * 1024 * 1024),
     )(ids_r, gate_r, back, dg)
     return mixed, tgrad, dg[None]
 
@@ -451,7 +493,7 @@
     cap = capacity_of(n_tok, topk, n_exp)
     hid = rest[2].shape[2]
     tiles = (
-        n_exp % GROUPS == 0 and n_sec == 4 and cap % 16 == 0 and n_tok % 128 == 0
+        n_exp == 2 * GROUPS and n_sec == 4 and cap % 16 == 0 and n_tok % 128 == 0
         and tokens.shape[1] % 128 == 0 and hid % (n_sec * 128) == 0
     )
     return (fused if tiles else local)(tokens, expert_ids, *rest)

time: 88.7 us -> 79.2 us (0.89)
  the two profiles are of different devices: /device:TPU:21 before, /device:TPU:0 now
where the time goes in v3:
time: 79.2 us; the launch traced here: 79.1 us
  Pallas kernels  78.4 us (99%)
    pallas_call x1, Pallas kernels, fused(): pl.pallas_call(functools.partial(expert_kernel, n_exp, cap), out_shape=(j...  74.2 us
    pallas_call x1, Pallas kernels, fused(): pl.pallas_call(functools.partial(combine_kernel, n_exp, cap), out_shape=(...  4.2 us

profile of v3, /device:TPU:0, one launch (start us, length us, event | category | flops | bytes accessed | tf_op | source)
XLA Modules:
  0.0 79.1 jit_solution(18252807378775007381)
XLA Ops:
  0.6 74.2 %shard_map.94 = (bf16[8,2,48,896]{3,2,1,0:T(8,128)(2,1)}, bf16[1024,896]{1,0:T(8,128)(2,1)}) custom-call(s32[2,128]{1,0:T(2,128)} %bitcast.9, f32[2,128]{1,0:T(2,128)} %bitcast.11, bf16[128,896]{1,0:T(8,128)(2,1)} %tok.1, bf16[128,896]{1,0:T(8,128)(2,1)} %cot.1, bf16[896,1024]{1,0:T(8,128)(2,1)} %bitcast.6, bf16[896,1024]{1,0:T(8,128)(2,1)} %bitcast.7, ...), custom_call_target="tpu_custom_call" | custom-call | tf_op jit(solution)/shard_map/pallas_call | solution.py:436
  74.9 4.2 %shard_map.95 = (bf16[128,896]{1,0:T(8,128)(2,1)}, bf16[128,896]{1,0:T(8,128)(2,1)}, bf16[1024,896]{1,0:T(8,128)(2,1)}) custom-call(s32[2,128]{1,0:T(2,128)} %bitcast.10, f32[2,128]{1,0:T(2,128)} %bitcast.12, bf16[8,2,48,896]{3,2,1,0:T(8,128)(2,1)} %get-tuple-element.8.back_h, bf16[1024,896]{1,0:T(8,128)(2,1)} %get-tuple-element.9.dg_h), custom_call_target="tpu_custom_call" | custom-call | tf_op jit(solution)/shard_map/pallas_call | solution.py:467

commit v4 on v3

--- a/solution.py
+++ b/solution.py
@@ -93,8 +93,8 @@
 DISPATCH = (2, 0, 1, 3)
 STEPS = (
     "A0", "B0", "A2", "B2", "C0", "C2", "A3", "D0", "B3", "D2",
-    "E2", "E0", "C3", "A1", "D3", "A4", "B1", "E3", "B4", "A5",
-    "C4", "B5", "C1", "D4", "C5", "E4", "D1", "D5", "E1", "E5",
+    "E2", "E0", "C3", "A1", "D3", "B1", "E3", "A4", "C1", "B4",
+    "A5", "D1", "C4", "B5", "E1", "D4", "C5", "E4", "D5", "E5",
 )
 NT = (((1,), (1,)), ((), ()))
 TN = (((0,), (0,)), ((), ()))

time: 79.2 us -> 76.1 us (0.961)
  Pallas kernels: 78.4 us -> 74.7 us
    pallas_call x1, Pallas kernels: 74.2 us -> 70.5 us  [fused(): pl.pallas_call(functools.partial(expert_kernel, n_exp, cap), out_shape=(j...]
where the time goes in v4:
time: 76.1 us; the launch traced here: 75.3 us
  Pallas kernels  74.7 us (98%)
    pallas_call x1, Pallas kernels, fused(): pl.pallas_call(functools.partial(expert_kernel, n_exp, cap), out_shape=(j...  70.5 us
    pallas_call x1, Pallas kernels, fused(): pl.pallas_call(functools.partial(combine_kernel, n_exp, cap), out_shape=(...  4.2 us

profile of v4, /device:TPU:0, one launch (start us, length us, event | category | flops | bytes accessed | tf_op | source)
XLA Modules:
  0.0 75.3 jit_solution(8575016698025784474)
XLA Ops:
  0.6 70.5 %shard_map.94 = (bf16[8,2,48,896]{3,2,1,0:T(8,128)(2,1)}, bf16[1024,896]{1,0:T(8,128)(2,1)}) custom-call(s32[2,128]{1,0:T(2,128)} %bitcast.9, f32[2,128]{1,0:T(2,128)} %bitcast.11, bf16[128,896]{1,0:T(8,128)(2,1)} %tok.1, bf16[128,896]{1,0:T(8,128)(2,1)} %cot.1, bf16[896,1024]{1,0:T(8,128)(2,1)} %bitcast.6, bf16[896,1024]{1,0:T(8,128)(2,1)} %bitcast.7, ...), custom_call_target="tpu_custom_call" | custom-call | tf_op jit(solution)/shard_map/pallas_call | solution.py:436
  71.1 4.2 %shard_map.95 = (bf16[128,896]{1,0:T(8,128)(2,1)}, bf16[128,896]{1,0:T(8,128)(2,1)}, bf16[1024,896]{1,0:T(8,128)(2,1)}) custom-call(s32[2,128]{1,0:T(2,128)} %bitcast.10, f32[2,128]{1,0:T(2,128)} %bitcast.12, bf16[8,2,48,896]{3,2,1,0:T(8,128)(2,1)} %get-tuple-element.8.back_h, bf16[1024,896]{1,0:T(8,128)(2,1)} %get-tuple-element.9.dg_h), custom_call_target="tpu_custom_call" | custom-call | tf_op jit(solution)/shard_map/pallas_call | solution.py:467
